TPU v7x, 32 devices: a whole 2x2x4 slice. The times are simulated.
32 devices in a mesh: row: 8 (over y, x, core), col: 4 (over z).
Axes of the slice: x: 2, y: 2, z: 4, core: 2. Of those that a mesh axis runs over, the one named last changes fastest.
Arguments:
- matrix: bfloat16 [3072, 3072], P('row', 'col'), may hold values from 3.2484531e-06 to 0.0012969971
- occ_matrix: int32 [24, 24], P('row', 'col'), may hold values 0 or 1
- batch: bfloat16 [3072, 512], P('row', 'col'), may hold values from 0.0099487305 to 4
- occ_batch: int32 [24, 4], P('row', 'col'), may hold values 0 or 1
- prune_mask: int32 [3072, 512], P('row', 'col'), may hold values 0 or 1
Outputs:
- clustered: float32 [3072, 512], P('row', 'col')
All inputs are finite; a program needn't handle non-finite values. No bound on the sum of `occ_matrix` or of `occ_batch` or of `prune_mask` on one device may be relied on, other than what follows from the above.
Results may differ from a plain program's by a relative error of at most 0.0003.
Values may be sent and summed in bfloat16 or wider, within the bound.
A program may use at most 64 MiB of HBM per device.

v0:
```python
import jax
import jax.numpy as jnp
from jax import lax
from jax.sharding import PartitionSpec as P


def expand_tiles(occupancy, size):
    return jnp.repeat(jnp.repeat(occupancy, size, axis=0), size, axis=1)


def body(matrix, occ_matrix, batch, occ_batch, prune_mask):
    tile_size = matrix.shape[0] // occ_matrix.shape[0]
    stored_matrix = matrix * expand_tiles(occ_matrix, tile_size).astype(jnp.bfloat16)
    stored_batch = batch * expand_tiles(occ_batch, tile_size).astype(jnp.bfloat16)
    whole_batch = lax.all_gather(stored_batch, "row", axis=0, tiled=True)
    expanded = jnp.dot(
        lax.all_gather(stored_matrix, "col", axis=1, tiled=True),
        whole_batch,
        preferred_element_type=jnp.float32,
    )
    kept = expanded * prune_mask.astype(jnp.float32)
    inflated = kept * kept
    col_total = lax.psum(jnp.sum(inflated, axis=0), "row")
    order = matrix.shape[0] * lax.axis_size("row")
    return inflated / (col_total[None, :] / order + 1e-05)


def solution(mesh):
    placed = (P("row", "col"), P("row", "col"), P("row", "col"), P("row", "col"), P("row", "col"))
    return jax.shard_map(
        body, mesh=mesh, in_specs=placed, out_specs=P("row", "col"), check_vma=False
    )
```

profile of v0, /device:TPU:0, one launch (start us, length us, event | category | flops | bytes accessed | tf_op | source)
XLA Modules:
  0.0 86.1 jit_solution(16578038678067250543)
XLA Ops:
  6.5 0.0 copy-start.2
  6.5 0.0 copy-start.1
  6.5 0.0 copy-start
  6.5 0.0 all-gather.2.cloned.1.call-start
  6.5 0.7 convert_element_type.25
  7.3 0.1 copy.6
  7.4 0.1 broadcast_bitcast_fusion
  7.5 1.4 %copy.7 = bf16[384,768]{0,1:T(8,128)(2,1)S(1)} copy(bf16[384,768]{1,0:T(8,128)(2,1)} %param.5) | data formatting | bytes 1179648 | tf_op args[0]
  8.8 0.9 %bitcast_multiply_fusion = bf16[384,768]{0,1:T(8,128)(2,1)} fusion(bf16[384,768]{0,1:T(8,128)(2,1)S(1)} %copy.7, bf16[384,6]{0,1:T(8,128)(2,1)S(1)} %bitcast.15), kind=kLoop, calls=%fused_computation.2 | loop fusion | flops 294912 | bytes 1184256 | tf_op jit(solution)/shard_map/mul | solution.py:13
  9.7 0.0 all-gather.2.cloned.1.call-update
  9.7 0.0 copy-done.2
  9.8 0.1 broadcast_bitcast_fusion.1
  9.8 0.0 copy-done.1
  9.8 0.1 broadcast_multiply_fusion
  10.0 11.9 %all_gather.7 = bf16[3072,128]{1,0:T(8,128)(2,1)S(1)} all-gather(bf16[384,128]{1,0:T(8,128)(2,1)S(1)} %broadcast_multiply_fusion), channel_id=1, replica_groups=mesh['row'=8,'col'=4] {'row'}, dimensions={0}, use_global_device_ids=true | all-gather | bytes 884736 | tf_op jit(solution)/shard_map/all_gather | solution.py:15
  21.8 40.8 %all-gather.2.cloned.1.call-done = bf16[384,3072]{0,1:T(8,128)(2,1)} async-done(((bf16[384,768]{0,1:T(8,128)(2,1)}), bf16[384,3072]{0,1:T(8,128)(2,1)}) %all-gather.2.cloned.1.call-update) | async-done | bytes 2359312 | tf_op jit(solution)/shard_map/all_gather | solution.py:17
  62.6 0.0 copy-done
  62.6 2.5 %fusion.1 = (f32[128]{0:T(128)S(1)}, f32[384,128]{1,0:T(8,128)S(1)}) fusion(s32[384,128]{1,0:T(8,128)S(1)} %copy-done, bf16[384,3072]{0,1:T(8,128)(2,1)} %all-gather.2.cloned.1.call-done, bf16[3072,128]{1,0:T(8,128)(2,1)S(1)} %all_gather.7), kind=kOutput, calls=%fused_computation.10 | convolution fusion | flops 302186368 | bytes 3539456 | tf_op jit(solution)/shard_map/dot_general | solution.py:16
  65.1 13.4 %psum.7 = f32[128]{0:T(128)S(1)} all-reduce(f32[128]{0:T(128)S(1)} %get-tuple-element.5), channel_id=1, replica_groups=mesh['row'=8,'col'=4] {'row'}, use_global_device_ids=true, to_apply=%region_1.0 | all-reduce | flops 128 | bytes 1024 | tf_op jit(solution)/shard_map/psum | solution.py:23
  78.5 0.7 broadcast_divide_fusion
  (3 shorter events, 0.0 us)
Async XLA Ops:
  6.5 3.2 %copy-start.2 = (s32[3,1]{0,1:T(1,128)S(1)}, s32[3,1]{0,1:T(1,128)}, u32[]{:S(2)}) copy-start(s32[3,1]{0,1:T(1,128)} %param.8) | copy-start | bytes 40
  6.5 3.3 %copy-start.1 = (bf16[384,128]{1,0:T(8,128)(2,1)S(1)}, bf16[384,128]{1,0:T(8,128)(2,1)}, u32[]{:S(2)}) copy-start(bf16[384,128]{1,0:T(8,128)(2,1)} %param.7) | copy-start | bytes 294916
  6.5 56.1 %copy-start = (s32[384,128]{1,0:T(8,128)S(1)}, s32[384,128]{1,0:T(8,128)}, u32[]{:S(2)}) copy-start(s32[384,128]{1,0:T(8,128)} %param.9) | copy-start | bytes 589828
  6.5 56.1 %all-gather.2.cloned.1.call-start = ((), (), s32[]{:S(2)}) async-start(), calls=%async_computation | async-start | bytes 2949120 | tf_op jit(solution)/shard_map/all_gather | solution.py:17
Sparse Core Ops, SparseCore 0:
  9.9 52.6 all-gather.1
where the time goes:
time: 86.3 us; the launch traced here: 86.1 us
  waiting for transfers between devices  40.8 us (47%)
  blocking collectives  25.3 us (29%)
  between operations  13.4 us (16%)
  matrix products  2.49 us (3%)
  other arithmetic  2.44 us (3%)
  local copies, waits for them, and re-layouts  1.64 us (2%)
    all_gather x1, waiting for transfers between devices, body(): lax.all_gather(stored_matrix, 'col', axis=1, tiled=True)  40.8 us
    psum x1, blocking collectives, body(): col_total = lax.psum(jnp.sum(inflated, axis=0), 'row')  13.4 us
    all_gather x1, blocking collectives, body(): whole_batch = lax.all_gather(stored_batch, 'row', axis=0, tiled=True)  11.9 us
    dot_general x1, matrix products, body(): jnp.dot(lax.all_gather(stored_matrix, 'col', axis=1, tiled=True), whole_b...  2.49 us
  transfers between devices with their start and end apart: 1, of which 1 were waited for; matrix products, arithmetic and copies ran while one was open for 0% of the time, Pallas kernels for 0%

commit v1 on v0

--- a/solution.py
+++ b/solution.py
@@ -20,7 +20,7 @@
     )
     kept = expanded * prune_mask.astype(jnp.float32)
     inflated = kept * kept
-    col_total = lax.psum(jnp.sum(inflated, axis=0), "row")
+    col_total = jnp.sum(lax.all_gather(jnp.sum(inflated, axis=0), "row"), axis=0)
     order = matrix.shape[0] * lax.axis_size("row")
     return inflated / (col_total[None, :] / order + 1e-05)
 

time: 86.3 us -> 81.6 us (0.946)
  blocking collectives: 25.3 us -> 20.6 us
    psum x1 -> x0, blocking collectives: 13.4 us -> none  [body(): col_total = lax.psum(jnp.sum(inflated, axis=0), 'row')]
    all_gather x0 -> x1, blocking collectives: none -> 8.75 us  [body(): lax.all_gather(jnp.sum(inflated, axis=0), 'row')]
where the time goes in v1:
time: 81.6 us; the launch traced here: 81.4 us
  waiting for transfers between devices  40.8 us (50%)
  blocking collectives  20.6 us (25%)
  between operations  13.4 us (16%)
  matrix products  2.49 us (3%)
  other arithmetic  2.46 us (3%)
  local copies, waits for them, and re-layouts  1.64 us (2%)
    all_gather x1, waiting for transfers between devices, body(): lax.all_gather(stored_matrix, 'col', axis=1, tiled=True)  40.8 us
    all_gather x1, blocking collectives, body(): whole_batch = lax.all_gather(stored_batch, 'row', axis=0, tiled=True)  11.9 us
    all_gather x1, blocking collectives, body(): lax.all_gather(jnp.sum(inflated, axis=0), 'row')  8.75 us
    dot_general x1, matrix products, body(): jnp.dot(lax.all_gather(stored_matrix, 'col', axis=1, tiled=True), whole_b...  2.49 us
  transfers between devices with their start and end apart: 1, of which 1 were waited for; matrix products, arithmetic and copies ran while one was open for 0% of the time, Pallas kernels for 0%

profile of v1, /device:TPU:0, one launch (start us, length us, event | category | flops | bytes accessed | tf_op | source)
XLA Modules:
  0.0 81.4 jit_solution(8353306862367518985)
XLA Ops:
  6.5 0.0 copy-start.2
  6.5 0.0 copy-start.1
  6.5 0.0 copy-start
  6.5 0.0 all-gather.4.cloned.1.call-start
  6.5 0.7 convert_element_type.25
  7.3 0.1 copy.8
  7.4 0.1 broadcast_bitcast_fusion
  7.5 1.4 %copy.9 = bf16[384,768]{0,1:T(8,128)(2,1)S(1)} copy(bf16[384,768]{1,0:T(8,128)(2,1)} %param.5) | data formatting | bytes 1179648 | tf_op args[0]
  8.8 0.9 %bitcast_multiply_fusion = bf16[384,768]{0,1:T(8,128)(2,1)} fusion(bf16[384,768]{0,1:T(8,128)(2,1)S(1)} %copy.9, bf16[384,6]{0,1:T(8,128)(2,1)S(1)} %bitcast.16), kind=kLoop, calls=%fused_computation.2 | loop fusion | flops 294912 | bytes 1184256 | tf_op jit(solution)/shard_map/mul | solution.py:13
  9.7 0.0 all-gather.4.cloned.1.call-update
  9.7 0.0 copy-done.2
  9.8 0.1 broadcast_bitcast_fusion.1
  9.8 0.0 copy-done.1
  9.8 0.1 broadcast_multiply_fusion
  10.0 11.9 %all_gather.13 = bf16[3072,128]{1,0:T(8,128)(2,1)S(1)} all-gather(bf16[384,128]{1,0:T(8,128)(2,1)S(1)} %broadcast_multiply_fusion), channel_id=1, replica_groups=mesh['row'=8,'col'=4] {'row'}, dimensions={0}, use_global_device_ids=true | all-gather | bytes 884736 | tf_op jit(solution)/shard_map/all_gather | solution.py:15
  21.8 40.8 %all-gather.4.cloned.1.call-done = bf16[384,3072]{0,1:T(8,128)(2,1)} async-done(((bf16[384,768]{0,1:T(8,128)(2,1)}), bf16[384,3072]{0,1:T(8,128)(2,1)}) %all-gather.4.cloned.1.call-update) | async-done | bytes 2359312 | tf_op jit(solution)/shard_map/all_gather | solution.py:17
  62.6 0.0 copy-done
  62.6 2.5 %fusion.1 = (f32[128]{0:T(128)S(1)}, f32[384,128]{1,0:T(8,128)S(1)}) fusion(s32[384,128]{1,0:T(8,128)S(1)} %copy-done, bf16[384,3072]{0,1:T(8,128)(2,1)} %all-gather.4.cloned.1.call-done, bf16[3072,128]{1,0:T(8,128)(2,1)S(1)} %all_gather.13), kind=kOutput, calls=%fused_computation.10 | convolution fusion | flops 302186368 | bytes 3539456 | tf_op jit(solution)/shard_map/dot_general | solution.py:16
  65.1 8.8 %all-gather.1 = f32[8,1,128]{2,1,0:T(1,128)S(1)} all-gather(f32[1,1,128]{2,1,0:T(1,128)S(1)} %bitcast.17), channel_id=2, replica_groups=mesh['row'=8,'col'=4] {'row'}, dimensions={0}, use_global_device_ids=true | all-gather | bytes 4608 | tf_op jit(solution)/shard_map/all_gather | solution.py:23
  73.9 0.7 broadcast_divide_fusion
  (4 shorter events, 0.0 us)
Async XLA Ops:
  6.5 3.2 %copy-start.2 = (s32[3,1]{0,1:T(1,128)S(1)}, s32[3,1]{0,1:T(1,128)}, u32[]{:S(2)}) copy-start(s32[3,1]{0,1:T(1,128)} %param.8) | copy-start | bytes 40
  6.5 3.3 %copy-start.1 = (bf16[384,128]{1,0:T(8,128)(2,1)S(1)}, bf16[384,128]{1,0:T(8,128)(2,1)}, u32[]{:S(2)}) copy-start(bf16[384,128]{1,0:T(8,128)(2,1)} %param.7) | copy-start | bytes 294916
  6.5 56.1 %copy-start = (s32[384,128]{1,0:T(8,128)S(1)}, s32[384,128]{1,0:T(8,128)}, u32[]{:S(2)}) copy-start(s32[384,128]{1,0:T(8,128)} %param.9) | copy-start | bytes 589828
  6.5 56.1 %all-gather.4.cloned.1.call-start = ((), (), s32[]{:S(2)}) async-start(), calls=%async_computation | async-start | bytes 2949120 | tf_op jit(solution)/shard_map/all_gather | solution.py:17
Sparse Core Ops, SparseCore 0:
  9.9 52.6 all-gather.3
